TPU v7x, 256 devices: a whole 4x4x8 slice. The times are simulated.
256 devices in a mesh: ctx: 32 (over z, x), ch: 8 (over y, core).
Axes of the slice: x: 4, y: 4, z: 8, core: 2. Of those that a mesh axis runs over, the one named last changes fastest.
Arguments:
- gate_q: bfloat16 [12288, 4096], P('ctx', 'ch'), may hold values from -6 to 6
- key_k: bfloat16 [12288, 4096], P('ctx', 'ch'), may hold values from -6 to 6
- value_v: bfloat16 [12288, 4096], P('ctx', 'ch'), may hold values from -6 to 6
- long_filter: bfloat16 [12288, 4096], P('ctx', 'ch'), may hold values from -0.0546875 to 0.0546875
- skip_gain: float32 [4096], P('ch'), may hold values from 0.5 to 1.5
- out_weight: bfloat16 [4096, 4096], P('ch'), may hold values from -0.125 to 0.125
Outputs:
- mixed: bfloat16 [12288, 4096], P('ctx', 'ch')
All inputs are finite; a program needn't handle non-finite values.
Results may differ from a plain program's by a relative error of at most 0.023.
Values may be sent and summed in bfloat16 or wider, within the bound.
A program may use at most 128 MiB of HBM per device.

v0:
```python
import math
import jax
import jax.numpy as jnp
from jax import lax
from jax.sharding import PartitionSpec as P


def for_sending(value):
    return jax.tree.map(lambda a: a.astype(jnp.bfloat16) if a.dtype == jnp.float32 else a, value)


def angle_table(left_index, right_index, length):
    turns = left_index[:, None] * right_index[None, :] % length
    angles = turns.astype(jnp.float32) * (2.0 * math.pi / length)
    return (jnp.cos(angles), jnp.sin(angles))


def local(gate_q, key_k, value_v, long_filter, skip_gain, out_weight):
    tok_rows, channels = key_k.shape
    group_count = lax.axis_size("ctx")
    position = lax.axis_index("ctx")
    block_rows = tok_rows // group_count
    full_len = 2 * group_count * tok_rows
    highest = lax.Precision.HIGHEST
    gated = (key_k.astype(jnp.float32) * value_v.astype(jnp.float32)).astype(jnp.bfloat16)
    freq_all = jnp.arange(2 * group_count, dtype=jnp.int32)
    block_index = jnp.arange(group_count, dtype=jnp.int32)
    row_index = jnp.arange(tok_rows, dtype=jnp.int32)
    cos_outer, sin_outer = angle_table(freq_all, block_index, 2 * group_count)
    cos_inner, sin_inner = angle_table(row_index, row_index, tok_rows)
    cos_final, sin_final = angle_table(block_index, freq_all, 2 * group_count)
    moved_gated, moved_filter = (
        lax.all_to_all(
            gated.reshape(group_count, block_rows, channels),
            "ctx",
            split_axis=0,
            concat_axis=0,
            tiled=True,
        ),
        lax.all_to_all(
            long_filter.reshape(group_count, block_rows, channels),
            "ctx",
            split_axis=0,
            concat_axis=0,
            tiled=True,
        ),
    )
    signals = jnp.stack([moved_gated, moved_filter]).astype(jnp.float32)
    outer_re = jnp.einsum("ka,sarc->skrc", cos_outer, signals, precision=highest)
    outer_im = -jnp.einsum("ka,sarc->skrc", sin_outer, signals, precision=highest)
    rows_here = position * block_rows + jnp.arange(block_rows, dtype=jnp.int32)
    twist_cos, twist_sin = angle_table(freq_all, rows_here, full_len)
    twist_cos = twist_cos[None, :, :, None]
    twist_sin = twist_sin[None, :, :, None]
    turned_re = outer_re * twist_cos + outer_im * twist_sin
    turned_im = outer_im * twist_cos - outer_re * twist_sin
    spectra = lax.all_to_all(
        jnp.stack([turned_re, turned_im], axis=1).astype(jnp.bfloat16),
        "ctx",
        split_axis=2,
        concat_axis=3,
        tiled=True,
    ).astype(jnp.float32)
    spec_re = jnp.einsum("kb,sebc->sekc", cos_inner, spectra[:, 0], precision=highest) + jnp.einsum(
        "kb,sebc->sekc", sin_inner, spectra[:, 1], precision=highest
    )
    spec_im = jnp.einsum("kb,sebc->sekc", cos_inner, spectra[:, 1], precision=highest) - jnp.einsum(
        "kb,sebc->sekc", sin_inner, spectra[:, 0], precision=highest
    )
    regrouped = lax.all_to_all(
        for_sending(jnp.stack([spec_re, spec_im])), "ctx", split_axis=3, concat_axis=2, tiled=True
    )
    ordered = jnp.swapaxes(regrouped, 2, 3)
    prod_re = ordered[0, 0] * ordered[0, 1] - ordered[1, 0] * ordered[1, 1]
    prod_im = ordered[0, 0] * ordered[1, 1] + ordered[1, 0] * ordered[0, 1]
    restored = lax.all_to_all(
        for_sending(jnp.swapaxes(jnp.stack([prod_re, prod_im]), 1, 2)),
        "ctx",
        split_axis=1,
        concat_axis=2,
        tiled=True,
    )
    prod_re = restored[0]
    prod_im = restored[1]
    back_re = jnp.einsum("bk,ekc->ebc", cos_inner, prod_re, precision=highest) - jnp.einsum(
        "bk,ekc->ebc", sin_inner, prod_im, precision=highest
    )
    back_im = jnp.einsum("bk,ekc->ebc", cos_inner, prod_im, precision=highest) + jnp.einsum(
        "bk,ekc->ebc", sin_inner, prod_re, precision=highest
    )
    own_freq = 2 * position + jnp.arange(2, dtype=jnp.int32)
    undo_cos, undo_sin = angle_table(own_freq, row_index, full_len)
    undo_cos = undo_cos[:, :, None]
    undo_sin = undo_sin[:, :, None]
    wound_re = back_re * undo_cos - back_im * undo_sin
    wound_im = back_im * undo_cos + back_re * undo_sin
    collected = lax.all_to_all(
        for_sending(jnp.stack([wound_re, wound_im])), "ctx", split_axis=2, concat_axis=1, tiled=True
    )
    finished = (
        jnp.einsum("ak,krc->arc", cos_final, collected[0], precision=highest)
        - jnp.einsum("ak,krc->arc", sin_final, collected[1], precision=highest)
    ) * (1.0 / full_len)
    arrived = lax.all_to_all(
        for_sending(finished), "ctx", split_axis=0, concat_axis=0, tiled=True
    ).astype(finished.dtype)
    conv = arrived.reshape(tok_rows, channels)
    hidden = (
        gate_q.astype(jnp.float32) * (conv + skip_gain[None, :] * gated.astype(jnp.float32))
    ).astype(jnp.bfloat16)
    terms = jnp.dot(hidden, out_weight, preferred_element_type=jnp.float32)
    return lax.psum_scatter(terms.astype(jnp.bfloat16), "ch", scatter_dimension=1, tiled=True)


def solution(mesh):
    placed = (
        P("ctx", "ch"),
        P("ctx", "ch"),
        P("ctx", "ch"),
        P("ctx", "ch"),
        P("ch"),
        P("ch", None),
    )
    return jax.shard_map(
        local, mesh=mesh, in_specs=placed, out_specs=P("ctx", "ch"), check_vma=False
    )
```

profile of v0, /device:TPU:2, one launch (start us, length us, event | category | flops | bytes accessed | tf_op | source)
XLA Modules:
  0.0 461.0 jit_solution(16877831459311176909)
XLA Ops:
  6.5 1.3 multiply_convert_fusion.1
  7.8 0.9 reshape.209
  8.7 11.6 %all-to-all-start = ((bf16[32,12,512]{2,1,0:T(8,128)(2,1)}), bf16[32,12,512]{2,1,0:T(8,128)(2,1)S(1)}, u32[]{:S(2)}, u32[]{:S(2)}) async-start(bf16[32,12,512]{2,1,0:T(8,128)(2,1)} %reshape.209), calls=%async_computation | async-start | bytes 1048576 | tf_op jit(solution)/shard_map/all_to_all | solution.py:33
  20.3 0.9 reshape.210
  21.2 15.9 %all-to-all-done = bf16[32,12,512]{2,1,0:T(8,128)(2,1)S(1)} async-done(((bf16[32,12,512]{2,1,0:T(8,128)(2,1)}), bf16[32,12,512]{2,1,0:T(8,128)(2,1)S(1)}, u32[]{:S(2)}, u32[]{:S(2)}) %all-to-all-start) | async-done | bytes 393248 | tf_op jit(solution)/shard_map/all_to_all | solution.py:33
  37.1 5.6 %all-to-all-start.1 = ((bf16[32,12,512]{2,1,0:T(8,128)(2,1)}), bf16[32,12,512]{2,1,0:T(8,128)(2,1)S(1)}, u32[]{:S(2)}, u32[]{:S(2)}) async-start(bf16[32,12,512]{2,1,0:T(8,128)(2,1)} %reshape.210), calls=%async_computation.1 | async-start | bytes 1048576 | tf_op jit(solution)/shard_map/all_to_all | solution.py:40
  43.1 15.5 %all-to-all-done.1 = bf16[32,12,512]{2,1,0:T(8,128)(2,1)S(1)} async-done(((bf16[32,12,512]{2,1,0:T(8,128)(2,1)}), bf16[32,12,512]{2,1,0:T(8,128)(2,1)S(1)}, u32[]{:S(2)}, u32[]{:S(2)}) %all-to-all-start.1) | async-done | bytes 393248 | tf_op jit(solution)/shard_map/all_to_all | solution.py:40
  58.9 1.7 fusion.47
  60.6 2.8 fusion.5
  63.7 3.2 copy.100
  67.0 77.9 %all_to_all.81 = bf16[2,2,64,12,512]{4,1,3,0,2:T(2,128)(2,1)S(1)} all-to-all(bf16[2,2,64,12,512]{4,1,3,0,2:T(2,128)(2,1)S(1)} %copy.100), channel_id=1, replica_groups=mesh['ctx'=32,'ch'=8] {'ctx'}, dimensions={2} | all-to-all | bytes 6291456 | tf_op jit(solution)/shard_map/all_to_all | solution.py:57
  144.8 3.2 copy.101
  148.1 3.1 fusion.152
  151.1 1.4 copy.126
  152.6 6.6 %fusion.10 = f32[2,2,512,384]{3,2,1,0:T(8,128)} fusion(bf16[2,1,2,384,512]{3,4,2,0,1:T(8,128)(2,1)S(1)} %copy.126), kind=kOutput, calls=%fused_computation.21 | convolution fusion | flops 3625205760 | bytes 4718592 | tf_op jit(solution)/shard_map/kb,sebc->sekc/dot_general | solution.py:64
  159.1 3.9 copy.127
  163.1 5.1 %fusion.6 = f32[2,2,512,384]{3,2,1,0:T(8,128)S(1)} fusion(bf16[2,1,2,384,512]{3,4,2,0,1:T(8,128)(2,1)S(1)} %copy.127), kind=kOutput, calls=%fused_computation.17 | convolution fusion | flops 3625205760 | bytes 4718592 | tf_op jit(solution)/shard_map/kb,sebc->sekc/dot_general | solution.py:67
  168.2 4.9 %fusion.12 = bf16[1,2,2,384,512]{3,4,2,1,0:T(8,128)(2,1)S(1)} fusion(f32[2,2,512,384]{3,2,1,0:T(8,128)S(1)} %copy-done, bf16[2,1,2,384,512]{3,4,2,0,1:T(8,128)(2,1)S(1)} %copy.127), kind=kOutput, calls=%fused_computation.27 | convolution fusion | flops 3626778624 | bytes 6291456 | tf_op jit(solution)/shard_map/kb,sebc->sekc/dot_general | solution.py:64
  173.2 5.3 %fusion.15 = bf16[1,2,2,384,512]{3,4,2,1,0:T(8,128)(2,1)S(1)} fusion(f32[2,2,512,384]{3,2,1,0:T(8,128)S(1)} %fusion.6, bf16[2,1,2,384,512]{3,4,2,0,1:T(8,128)(2,1)S(1)} %copy.126), kind=kOutput, calls=%fused_computation.28 | convolution fusion | flops 3626778624 | bytes 6291456 | tf_op jit(solution)/shard_map/kb,sebc->sekc/dot_general | solution.py:67
  178.8 6.0 %copy.104 = bf16[2,2,2,384,512]{4,2,1,0,3:T(2,128)(2,1)} copy(bf16[2,2,2,384,512]{3,4,2,1,0:T(8,128)(2,1)S(1)} %pad_maximum_fusion.1) | data formatting | bytes 6291456 | tf_op jit(solution)/shard_map/stack | solution.py:71
  184.9 77.1 %all_to_all.82 = bf16[2,2,2,384,512]{4,2,1,0,3:T(2,128)(2,1)S(1)} all-to-all(bf16[2,2,2,384,512]{4,2,1,0,3:T(2,128)(2,1)} %copy.104), channel_id=1, replica_groups=mesh['ctx'=32,'ch'=8] {'ctx'}, dimensions={3} | all-to-all | bytes 6291456 | tf_op jit(solution)/shard_map/all_to_all | solution.py:70
  262.0 3.5 copy.106
  265.6 6.1 %multiply_subtract_fusion = (bf16[1,1,12,64,512]{4,1,2,3,0:T(2,128)(2,1)S(1)}, bf16[1,1,12,64,512]{4,1,2,3,0:T(2,128)(2,1)S(1)}) fusion(bf16[2,2,12,64,512]{4,1,2,3,0:T(2,128)(2,1)S(1)} %bitcast.145), kind=kLoop, calls=%fused_computation.26 | loop fusion | flops 2359296 | bytes 4718592 | tf_op jit(solution)/shard_map/sub | solution.py:74
  271.7 0.9 copy_bitcast_fusion
  272.7 2.8 copy.109
  275.5 5.6 %all-to-all-start.4 = ((bf16[2,64,12,512]{3,0,2,1:T(2,128)(2,1)}), bf16[2,64,12,512]{3,0,2,1:T(2,128)(2,1)S(1)}, u32[]{:S(2)}, u32[]{:S(2)}) async-start(bf16[2,64,12,512]{3,0,2,1:T(2,128)(2,1)} %copy.109), calls=%async_computation.4 | async-start | bytes 3145728 | tf_op jit(solution)/shard_map/all_to_all | solution.py:76
  281.1 0.4 reduce-scatter.2.cloned.1.call-start
  281.7 36.4 %all-to-all-done.4 = bf16[2,64,12,512]{3,0,2,1:T(2,128)(2,1)S(1)} async-done(((bf16[2,64,12,512]{3,0,2,1:T(2,128)(2,1)}), bf16[2,64,12,512]{3,0,2,1:T(2,128)(2,1)S(1)}, u32[]{:S(2)}, u32[]{:S(2)}) %all-to-all-start.4) | async-done | bytes 1572896 | tf_op jit(solution)/shard_map/all_to_all | solution.py:76
  318.2 3.6 fusion.154
  321.8 0.8 copy.112
  322.6 0.7 copy.113
  323.3 4.9 %fusion.26 = f32[2,512,384]{2,1,0:T(8,128)} fusion(bf16[2,384,512]{1,2,0:T(8,128)(2,1)S(1)} %copy.113), kind=kOutput, calls=%fused_computation.46 | convolution fusion | flops 1813266432 | bytes 2359296 | tf_op jit(solution)/shard_map/bk,ekc->ebc/dot_general | solution.py:88
  328.2 0.8 copy.110
  329.0 0.9 copy.111
  329.9 3.7 fusion.28
  333.7 3.7 convolution_add_fusion
  337.4 4.8 %fusion.20 = (bf16[1,2,384,512]{2,3,1,0:T(8,128)(2,1)S(1)}, bf16[1,2,384,512]{2,3,1,0:T(8,128)(2,1)S(1)}) fusion(f32[2,512,384]{2,1,0:T(8,128)S(1)} %convolution_add_fusion, f32[2,384]{1,0:T(2,128)S(1)} %get-tuple-element.18, f32[2,384]{1,0:T(2,128)S(1)} %get-tuple-element.17, f32[2,512,384]{2,1,0:T(8,128)S(1)} %fusion.28, bf16[2,384,512]{1,2,0:T(8,128)(2,1)S(1)} %copy.113), kind=kOutput, calls=%fused_computation.35 | convolution fusion | flops 1816805376 | bytes 5511168 | tf_op jit(solution)/shard_map/bk,ekc->ebc/dot_general | solution.py:85
  342.3 1.6 copy.116
  344.0 43.3 %all_to_all.83 = bf16[2,2,384,512]{3,1,0,2:T(2,128)(2,1)S(1)} all-to-all(bf16[2,2,384,512]{3,1,0,2:T(2,128)(2,1)S(1)} %copy.116), channel_id=1, replica_groups=mesh['ctx'=32,'ch'=8] {'ctx'}, dimensions={2} | all-to-all | bytes 3145728 | tf_op jit(solution)/shard_map/all_to_all | solution.py:97
  387.3 1.1 copy.117
  388.4 1.1 fusion.153
  389.5 0.7 copy.118
  390.5 0.5 fusion.83
  391.0 0.7 copy.119
  392.0 0.5 fusion.19
  392.8 20.0 %all_to_all.84 = bf16[32,12,512]{2,1,0:T(8,128)(2,1)S(1)} all-to-all(bf16[32,12,512]{2,1,0:T(8,128)(2,1)S(1)} %copy.120), channel_id=1, replica_groups=mesh['ctx'=32,'ch'=8] {'ctx'}, dimensions={0} | all-to-all | bytes 786432 | tf_op jit(solution)/shard_map/all_to_all | solution.py:104
  412.9 5.7 %convolution_convert_fusion = bf16[384,4096]{1,0:T(8,128)(2,1)} fusion(bf16[512,4096]{1,0:T(8,128)(2,1)} %param.11, f32[384,512]{1,0:T(8,128)S(1)} %reshape.214, bf16[384,512]{1,0:T(8,128)(2,1)S(1)} %multiply_convert_fusion.1, bf16[384,512]{1,0:T(8,128)(2,1)S(1)} %copy-done.3, f32[512]{0:T(512)S(1)} %copy-done.4), kind=kOutput, calls=%fused_computation | convolution fusion | flops 1613365248 | bytes 8914944 | tf_op jit(solution)/shard_map/dot_general | solution.py:111
  418.6 35.4 %reduce-scatter.2.cloned.1.call-done = bf16[384,512]{1,0:T(8,128)(2,1)} async-done(((bf16[384,4096]{1,0:T(8,128)(2,1)}), bf16[384,512]{1,0:T(8,128)(2,1)}) %reduce-scatter.2.cloned.1.call-update) | async-done | bytes 393232 | tf_op jit(solution)/shard_map/reduce_scatter | solution.py:112
  (25 shorter events, 2.6 us)
Async XLA Ops:
  6.5 13.8 %copy-start.2 = (bf16[384,512]{1,0:T(8,128)(2,1)S(1)}, bf16[384,512]{1,0:T(8,128)(2,1)}, u32[]{:S(2)}) copy-start(bf16[384,512]{1,0:T(8,128)(2,1)} %param.9) | copy-start | bytes 1179652
  8.7 28.5 %all-to-all-start = ((bf16[32,12,512]{2,1,0:T(8,128)(2,1)}), bf16[32,12,512]{2,1,0:T(8,128)(2,1)S(1)}, u32[]{:S(2)}, u32[]{:S(2)}) async-start(bf16[32,12,512]{2,1,0:T(8,128)(2,1)} %reshape.209), calls=%async_computation | async-start | bytes 1048576 | tf_op jit(solution)/shard_map/all_to_all | solution.py:33
  37.1 21.5 %all-to-all-start.1 = ((bf16[32,12,512]{2,1,0:T(8,128)(2,1)}), bf16[32,12,512]{2,1,0:T(8,128)(2,1)S(1)}, u32[]{:S(2)}, u32[]{:S(2)}) async-start(bf16[32,12,512]{2,1,0:T(8,128)(2,1)} %reshape.210), calls=%async_computation.1 | async-start | bytes 1048576 | tf_op jit(solution)/shard_map/all_to_all | solution.py:40
  163.1 5.2 %copy-start = (f32[2,2,512,384]{3,2,1,0:T(8,128)S(1)}, f32[2,2,512,384]{3,2,1,0:T(8,128)}, u32[]{:S(2)}) copy-start(f32[2,2,512,384]{3,2,1,0:T(8,128)} %fusion.10) | copy-start | bytes 9437188
  275.5 42.6 %all-to-all-start.4 = ((bf16[2,64,12,512]{3,0,2,1:T(2,128)(2,1)}), bf16[2,64,12,512]{3,0,2,1:T(2,128)(2,1)S(1)}, u32[]{:S(2)}, u32[]{:S(2)}) async-start(bf16[2,64,12,512]{3,0,2,1:T(2,128)(2,1)} %copy.109), calls=%async_computation.4 | async-start | bytes 3145728 | tf_op jit(solution)/shard_map/all_to_all | solution.py:76
  281.1 172.8 %reduce-scatter.2.cloned.1.call-start = ((), (), s32[]{:S(2)}) async-start(), calls=%async_computation.8 | async-start | bytes 3538944 | tf_op jit(solution)/shard_map/reduce_scatter | solution.py:112
  329.9 3.7 copy-start.1
  392.6 20.3 %copy-start.3 = (bf16[384,512]{1,0:T(8,128)(2,1)S(1)}, bf16[384,512]{1,0:T(8,128)(2,1)}, u32[]{:S(2)}) copy-start(bf16[384,512]{1,0:T(8,128)(2,1)} %param.6) | copy-start | bytes 1179652
  392.6 20.3 %copy-start.4 = (f32[512]{0:T(512)S(1)}, f32[512]{0:T(512)}, u32[]{:S(2)}) copy-start(f32[512]{0:T(512)} %param.10) | copy-start | bytes 6148
Sparse Core Ops, SparseCore 0:
  418.7 35.2 reduce-scatter.1
where the time goes:
time: 468 us; the launch traced here: 461 us
  blocking collectives  218 us (47%)
  waiting for transfers between devices  103 us (22%)
  matrix products  50.4 us (11%)
  local copies, waits for them, and re-layouts  43.2 us (9%)
  starting transfers between devices  23.2 us (5%)
  between operations  14 us (3%)
  other arithmetic  8.66 us (2%)
    all_to_all x1, blocking collectives, local(): lax.all_to_all(jnp.stack([turned_re, turned_im], axis=1).astype(jnp.bfloa...  77.9 us
    all_to_all x1, blocking collectives, local(): lax.all_to_all(for_sending(jnp.stack([spec_re, spec_im])), 'ctx', split_a...  77.1 us
    all_to_all x1, blocking collectives, local(): lax.all_to_all(for_sending(jnp.stack([wound_re, wound_im])), 'ctx', split...  43.3 us
    all_to_all x1, waiting for transfers between devices, local(): lax.all_to_all(for_sending(jnp.swapaxes(jnp.stack([prod_re, prod_im]), 1,...  36.4 us
    reduce_scatter x1, waiting for transfers between devices, local(): lax.psum_scatter(terms.astype(jnp.bfloat16), 'ch', scatter_dimension=1, t...  35.4 us
    all_to_all x1, blocking collectives, local(): lax.all_to_all(for_sending(finished), 'ctx', split_axis=0, concat_axis=0,...  20 us
    all_to_all x1, waiting for transfers between devices, local(): lax.all_to_all(gated.reshape(group_count, block_rows, channels), 'ctx', s...  15.9 us
    all_to_all x1, waiting for transfers between devices, local(): lax.all_to_all(long_filter.reshape(group_count, block_rows, channels), 'c...  15.5 us
  transfers between devices with their start and end apart: 4, of which 4 were waited for; matrix products, arithmetic and copies ran while one was open for 0% of the time, Pallas kernels for 0%

commit v1 on v0

--- a/solution.py
+++ b/solution.py
@@ -67,8 +67,16 @@
     spec_im = jnp.einsum("kb,sebc->sekc", cos_inner, spectra[:, 1], precision=highest) - jnp.einsum(
         "kb,sebc->sekc", sin_inner, spectra[:, 0], precision=highest
     )
-    regrouped = lax.all_to_all(
-        for_sending(jnp.stack([spec_re, spec_im])), "ctx", split_axis=3, concat_axis=2, tiled=True
+    regrouped = jnp.concatenate(
+        lax.all_to_all(
+            jnp.stack(
+                jnp.split(for_sending(jnp.stack([spec_re, spec_im])), lax.axis_size("ctx"), axis=3)
+            ),
+            "ctx",
+            0,
+            0,
+        ),
+        axis=2,
     )
     ordered = jnp.swapaxes(regrouped, 2, 3)
     prod_re = ordered[0, 0] * ordered[0, 1] - ordered[1, 0] * ordered[1, 1]

time: 468 us -> 462 us (0.987)
  local copies, waits for them, and re-layouts: 43.2 us -> 37.7 us
    unnamed x12 -> x8, local copies, waits for them, and re-layouts: 5.35 us -> 0.02 us
where the time goes in v1:
time: 462 us; the launch traced here: 455 us
  blocking collectives  218 us (47%)
  waiting for transfers between devices  104 us (23%)
  matrix products  49.1 us (11%)
  local copies, waits for them, and re-layouts  37.7 us (8%)
  starting transfers between devices  22.8 us (5%)
  between operations  14.5 us (3%)
  other arithmetic  9.09 us (2%)
    all_to_all x1, blocking collectives, local(): lax.all_to_all(jnp.stack([turned_re, turned_im], axis=1).astype(jnp.bfloa...  77.6 us
    all_to_all x1, blocking collectives, local(): lax.all_to_all(jnp.stack(jnp.split(for_sending(jnp.stack([spec_re, spec_i...  76.9 us
    all_to_all x1, blocking collectives, local(): lax.all_to_all(for_sending(jnp.stack([wound_re, wound_im])), 'ctx', split...  43.4 us
    all_to_all x1, waiting for transfers between devices, local(): lax.all_to_all(for_sending(jnp.swapaxes(jnp.stack([prod_re, prod_im]), 1,...  36.9 us
    reduce_scatter x1, waiting for transfers between devices, local(): lax.psum_scatter(terms.astype(jnp.bfloat16), 'ch', scatter_dimension=1, t...  35.3 us
    all_to_all x1, blocking collectives, local(): lax.all_to_all(for_sending(finished), 'ctx', split_axis=0, concat_axis=0,...  19.9 us
    all_to_all x1, waiting for transfers between devices, local(): lax.all_to_all(gated.reshape(group_count, block_rows, channels), 'ctx', s...  15.9 us
    all_to_all x1, waiting for transfers between devices, local(): lax.all_to_all(long_filter.reshape(group_count, block_rows, channels), 'c...  15.5 us
  transfers between devices with their start and end apart: 4, of which 4 were waited for; matrix products, arithmetic and copies ran while one was open for 0% of the time, Pallas kernels for 0%

profile of v1, /device:TPU:2, one launch (start us, length us, event | category | flops | bytes accessed | tf_op | source)
XLA Modules:
  0.0 454.8 jit_solution(8927652447015515321)
XLA Ops:
  6.5 1.3 multiply_convert_fusion.1
  7.8 0.9 reshape.215
  8.7 11.6 %all-to-all-start = ((bf16[32,12,512]{2,1,0:T(8,128)(2,1)}), bf16[32,12,512]{2,1,0:T(8,128)(2,1)S(1)}, u32[]{:S(2)}, u32[]{:S(2)}) async-start(bf16[32,12,512]{2,1,0:T(8,128)(2,1)} %reshape.215), calls=%async_computation | async-start | bytes 1048576 | tf_op jit(solution)/shard_map/all_to_all | solution.py:33
  20.3 0.9 reshape.216
  21.2 15.9 %all-to-all-done = bf16[32,12,512]{2,1,0:T(8,128)(2,1)S(1)} async-done(((bf16[32,12,512]{2,1,0:T(8,128)(2,1)}), bf16[32,12,512]{2,1,0:T(8,128)(2,1)S(1)}, u32[]{:S(2)}, u32[]{:S(2)}) %all-to-all-start) | async-done | bytes 393248 | tf_op jit(solution)/shard_map/all_to_all | solution.py:33
  37.1 5.6 %all-to-all-start.1 = ((bf16[32,12,512]{2,1,0:T(8,128)(2,1)}), bf16[32,12,512]{2,1,0:T(8,128)(2,1)S(1)}, u32[]{:S(2)}, u32[]{:S(2)}) async-start(bf16[32,12,512]{2,1,0:T(8,128)(2,1)} %reshape.216), calls=%async_computation.1 | async-start | bytes 1048576 | tf_op jit(solution)/shard_map/all_to_all | solution.py:40
  43.1 15.5 %all-to-all-done.1 = bf16[32,12,512]{2,1,0:T(8,128)(2,1)S(1)} async-done(((bf16[32,12,512]{2,1,0:T(8,128)(2,1)}), bf16[32,12,512]{2,1,0:T(8,128)(2,1)S(1)}, u32[]{:S(2)}, u32[]{:S(2)}) %all-to-all-start.1) | async-done | bytes 393248 | tf_op jit(solution)/shard_map/all_to_all | solution.py:40
  58.9 1.7 fusion.39
  60.6 2.8 fusion.5
  63.4 0.3 pad_maximum_fusion
  63.7 3.2 copy.96
  67.0 77.6 %all_to_all.68 = bf16[2,2,64,12,512]{4,1,3,0,2:T(2,128)(2,1)S(1)} all-to-all(bf16[2,2,64,12,512]{4,1,3,0,2:T(2,128)(2,1)S(1)} %copy.96), channel_id=1, replica_groups=mesh['ctx'=32,'ch'=8] {'ctx'}, dimensions={2} | all-to-all | bytes 6291456 | tf_op jit(solution)/shard_map/all_to_all | solution.py:57
  144.6 3.2 copy.97
  147.8 2.2 fusion.177
  150.0 5.1 %fusion.8 = f32[2,2,512,384]{2,3,1,0:T(8,128)S(1)} fusion(bf16[2,1,2,384,512]{4,2,3,1,0:T(2,128)(2,1)S(1)} %get-tuple-element.11), kind=kOutput, calls=%fused_computation.88 | convolution fusion | flops 3625205760 | bytes 4718592 | tf_op jit(solution)/shard_map/kb,sebc->sekc/dot_general | solution.py:64
  155.1 5.1 %fusion.9 = f32[2,2,512,384]{2,3,1,0:T(8,128)S(1)} fusion(bf16[2,1,2,384,512]{4,2,3,1,0:T(2,128)(2,1)S(1)} %get-tuple-element.12), kind=kOutput, calls=%fused_computation.89 | convolution fusion | flops 3625205760 | bytes 4718592 | tf_op jit(solution)/shard_map/kb,sebc->sekc/dot_general | solution.py:67
  160.2 5.5 %fusion.6 = bf16[1,2,2,384,512]{4,3,2,1,0:T(8,128)(2,1)S(1)} fusion(f32[2,2,512,384]{2,3,1,0:T(8,128)S(1)} %fusion.8, bf16[2,1,2,384,512]{4,2,3,1,0:T(2,128)(2,1)S(1)} %get-tuple-element.12), kind=kOutput, calls=%fused_computation.84 | convolution fusion | flops 3626778624 | bytes 6291456 | tf_op jit(solution)/shard_map/kb,sebc->sekc/dot_general | solution.py:64
  165.7 5.1 %fusion.7 = bf16[1,2,2,384,512]{4,3,2,1,0:T(8,128)(2,1)S(1)} fusion(f32[2,2,512,384]{2,3,1,0:T(8,128)S(1)} %fusion.9, bf16[2,1,2,384,512]{4,2,3,1,0:T(2,128)(2,1)S(1)} %get-tuple-element.11), kind=kOutput, calls=%fused_computation.85 | convolution fusion | flops 3626778624 | bytes 6291456 | tf_op jit(solution)/shard_map/kb,sebc->sekc/dot_general | solution.py:67
  171.8 6.5 %copy.100 = bf16[32,2,2,2,12,512]{5,3,4,2,1,0:T(2,128)(2,1)S(1)} copy(bf16[32,2,2,2,12,512]{5,4,3,2,1,0:T(8,128)(2,1)S(1)} %fusion.98) | data formatting | bytes 6291456 | tf_op jit(solution)/shard_map/stack | solution.py:72
  178.3 76.9 %all_to_all.69 = bf16[32,2,2,2,12,512]{5,3,4,2,1,0:T(2,128)(2,1)S(1)} all-to-all(bf16[32,2,2,2,12,512]{5,3,4,2,1,0:T(2,128)(2,1)S(1)} %copy.100), channel_id=1, replica_groups=mesh['ctx'=32,'ch'=8] {'ctx'}, dimensions={0} | all-to-all | bytes 6291456 | tf_op jit(solution)/shard_map/all_to_all | solution.py:71
  255.2 3.5 copy.101
  258.7 6.1 %multiply_subtract_fusion = (bf16[1,1,12,64,512]{4,1,2,3,0:T(2,128)(2,1)S(1)}, bf16[1,1,12,64,512]{4,1,2,3,0:T(2,128)(2,1)S(1)}) fusion(bf16[2,2,12,64,512]{4,1,2,3,0:T(2,128)(2,1)S(1)} %bitcast.203), kind=kLoop, calls=%fused_computation.83 | loop fusion | flops 2359296 | bytes 4718592 | tf_op jit(solution)/shard_map/sub | solution.py:82
  264.9 0.9 copy_bitcast_fusion.6
  265.9 2.8 copy.104
  268.7 5.6 %all-to-all-start.4 = ((bf16[2,64,12,512]{3,0,2,1:T(2,128)(2,1)}), bf16[2,64,12,512]{3,0,2,1:T(2,128)(2,1)S(1)}, u32[]{:S(2)}, u32[]{:S(2)}) async-start(bf16[2,64,12,512]{3,0,2,1:T(2,128)(2,1)} %copy.104), calls=%async_computation.4 | async-start | bytes 3145728 | tf_op jit(solution)/shard_map/all_to_all | solution.py:84
  274.5 36.9 %all-to-all-done.4 = bf16[2,64,12,512]{3,0,2,1:T(2,128)(2,1)S(1)} async-done(((bf16[2,64,12,512]{3,0,2,1:T(2,128)(2,1)}), bf16[2,64,12,512]{3,0,2,1:T(2,128)(2,1)S(1)}, u32[]{:S(2)}, u32[]{:S(2)}) %all-to-all-start.4) | async-done | bytes 1572896 | tf_op jit(solution)/shard_map/all_to_all | solution.py:84
  311.4 3.8 fusion.179
  315.2 0.8 copy.107
  316.0 0.7 copy.108
  316.7 4.9 %fusion.18 = f32[2,512,384]{2,1,0:T(8,128)} fusion(bf16[2,384,512]{1,2,0:T(8,128)(2,1)S(1)} %copy.108), kind=kOutput, calls=%fused_computation.105 | convolution fusion | flops 1813266432 | bytes 2359296 | tf_op jit(solution)/shard_map/bk,ekc->ebc/dot_general | solution.py:96
  321.6 0.8 copy.105
  322.5 1.0 copy.106
  323.4 3.7 fusion.20
  327.2 3.7 convolution_add_fusion
  330.9 4.8 %fusion.12 = (bf16[1,2,384,512]{2,3,1,0:T(8,128)(2,1)S(1)}, bf16[1,2,384,512]{2,3,1,0:T(8,128)(2,1)S(1)}) fusion(f32[2,512,384]{2,1,0:T(8,128)S(1)} %convolution_add_fusion, f32[2,384]{1,0:T(2,128)S(1)} %get-tuple-element.18, f32[2,384]{1,0:T(2,128)S(1)} %get-tuple-element.17, f32[2,512,384]{2,1,0:T(8,128)S(1)} %fusion.20, bf16[2,384,512]{1,2,0:T(8,128)(2,1)S(1)} %copy.108), kind=kOutput, calls=%fused_computation.94 | convolution fusion | flops 1816805376 | bytes 5511168 | tf_op jit(solution)/shard_map/bk,ekc->ebc/dot_general | solution.py:93
  335.9 1.6 copy.111
  337.5 43.4 %all_to_all.70 = bf16[2,2,384,512]{3,1,0,2:T(2,128)(2,1)S(1)} all-to-all(bf16[2,2,384,512]{3,1,0,2:T(2,128)(2,1)S(1)} %copy.111), channel_id=1, replica_groups=mesh['ctx'=32,'ch'=8] {'ctx'}, dimensions={2} | all-to-all | bytes 3145728 | tf_op jit(solution)/shard_map/all_to_all | solution.py:105
  380.9 1.1 copy.112
  382.0 1.1 fusion.178
  383.1 0.7 copy.113
  383.7 0.3 squeeze.32
  384.0 0.5 fusion.108
  384.6 0.7 copy.114
  385.3 0.3 squeeze.33
  385.6 0.5 fusion.11
  386.4 19.9 %all_to_all.71 = bf16[32,12,512]{2,1,0:T(8,128)(2,1)S(1)} all-to-all(bf16[32,12,512]{2,1,0:T(8,128)(2,1)S(1)} %copy.115), channel_id=1, replica_groups=mesh['ctx'=32,'ch'=8] {'ctx'}, dimensions={0} | all-to-all | bytes 786432 | tf_op jit(solution)/shard_map/all_to_all | solution.py:112
  406.4 5.6 %convolution_convert_fusion = bf16[384,4096]{1,0:T(8,128)(2,1)} fusion(bf16[512,4096]{1,0:T(8,128)(2,1)} %param.11, f32[384,512]{1,0:T(8,128)S(1)} %reshape.222, bf16[384,512]{1,0:T(8,128)(2,1)S(1)} %multiply_convert_fusion.1, bf16[384,512]{1,0:T(8,128)(2,1)S(1)} %copy-done.2, f32[512]{0:T(512)S(1)} %copy-done.3), kind=kOutput, calls=%fused_computation.62 | convolution fusion | flops 1613365248 | bytes 8914944 | tf_op jit(solution)/shard_map/dot_general | solution.py:119
  412.1 35.3 %reduce-scatter.2.cloned.1.call-done = bf16[384,512]{1,0:T(8,128)(2,1)} async-done(((bf16[384,4096]{1,0:T(8,128)(2,1)}), bf16[384,512]{1,0:T(8,128)(2,1)}) %reduce-scatter.2.cloned.1.call-update) | async-done | bytes 393232 | tf_op jit(solution)/shard_map/reduce_scatter | solution.py:120
  (52 shorter events, 2.2 us)
Async XLA Ops:
  6.5 13.8 %copy-start.1 = (bf16[384,512]{1,0:T(8,128)(2,1)S(1)}, bf16[384,512]{1,0:T(8,128)(2,1)}, u32[]{:S(2)}) copy-start(bf16[384,512]{1,0:T(8,128)(2,1)} %param.9) | copy-start | bytes 1179652
  8.7 28.5 %all-to-all-start = ((bf16[32,12,512]{2,1,0:T(8,128)(2,1)}), bf16[32,12,512]{2,1,0:T(8,128)(2,1)S(1)}, u32[]{:S(2)}, u32[]{:S(2)}) async-start(bf16[32,12,512]{2,1,0:T(8,128)(2,1)} %reshape.215), calls=%async_computation | async-start | bytes 1048576 | tf_op jit(solution)/shard_map/all_to_all | solution.py:33
  37.1 21.5 %all-to-all-start.1 = ((bf16[32,12,512]{2,1,0:T(8,128)(2,1)}), bf16[32,12,512]{2,1,0:T(8,128)(2,1)S(1)}, u32[]{:S(2)}, u32[]{:S(2)}) async-start(bf16[32,12,512]{2,1,0:T(8,128)(2,1)} %reshape.216), calls=%async_computation.1 | async-start | bytes 1048576 | tf_op jit(solution)/shard_map/all_to_all | solution.py:40
  268.7 42.7 %all-to-all-start.4 = ((bf16[2,64,12,512]{3,0,2,1:T(2,128)(2,1)}), bf16[2,64,12,512]{3,0,2,1:T(2,128)(2,1)S(1)}, u32[]{:S(2)}, u32[]{:S(2)}) async-start(bf16[2,64,12,512]{3,0,2,1:T(2,128)(2,1)} %copy.104), calls=%async_computation.4 | async-start | bytes 3145728 | tf_op jit(solution)/shard_map/all_to_all | solution.py:84
  274.3 173.1 %reduce-scatter.2.cloned.1.call-start = ((), (), s32[]{:S(2)}) async-start(), calls=%async_computation.8 | async-start | bytes 3538944 | tf_op jit(solution)/shard_map/reduce_scatter | solution.py:120
  323.4 3.7 copy-start
  385.3 21.1 %copy-start.2 = (bf16[384,512]{1,0:T(8,128)(2,1)S(1)}, bf16[384,512]{1,0:T(8,128)(2,1)}, u32[]{:S(2)}) copy-start(bf16[384,512]{1,0:T(8,128)(2,1)} %param.6) | copy-start | bytes 1179652
  385.3 21.1 %copy-start.3 = (f32[512]{0:T(512)S(1)}, f32[512]{0:T(512)}, u32[]{:S(2)}) copy-start(f32[512]{0:T(512)} %param.10) | copy-start | bytes 6148
Sparse Core Ops, SparseCore 0:
  412.2 35.1 reduce-scatter.1
